TPU v7x, 32 devices: a whole 2x2x4 slice. The times are simulated.
32 devices in a mesh: groups: 2 (over y), rows: 8 (over z, x), layers: 2 (over core).
Axes of the slice: x: 2, y: 2, z: 4, core: 2. Of those that a mesh axis runs over, the one named last changes fastest.
Arguments:
- train_grads: bfloat16 [6144, 2, 4096], P(('groups', 'rows'), 'layers'), parts along dimension 0, may hold values from -6 to 6
- query_grads: bfloat16 [2, 2048, 4096], P('layers', ('groups', 'rows')), parts along dimension 1, may hold values from -0.09375 to 0.09375
Outputs:
- scores: float32 [1024, 6144], P('layers', ('groups', 'rows')), parts along dimension 1
There are 2 independent parts, one for each index of `groups`. A program takes and returns all parts, laid end to end along the dimension named above; each array names one. Nothing has to cross between parts.
All inputs are finite; a program needn't handle non-finite values.
Results may differ from a plain program's by a relative error of at most 0.0003.
Values may be sent and summed in bfloat16 or wider, within the bound.
No kernel may reach another device: no remote copies, remote signals or barrier semaphores. Data moves between devices by JAX's collectives and lax.ppermute only.
A program may use at most 64 MiB of HBM per device.

v0:
```python
import jax
import jax.numpy as jnp
from jax import lax
from jax.sharding import PartitionSpec as P


def partial_scores(queries, train_grads):
    return jnp.einsum("lqk,nlk->qn", queries, train_grads, preferred_element_type=jnp.float32)


def shards(train_grads, query_grads):
    terms = partial_scores(lax.all_gather(query_grads, "rows", axis=1, tiled=True), train_grads)
    return lax.psum_scatter(terms, "layers", scatter_dimension=0, tiled=True)


def solution(mesh):
    in_specs = (P(("groups", "rows"), "layers", None), P("layers", ("groups", "rows"), None))
    out_specs = P("layers", ("groups", "rows"))
    return jax.shard_map(shards, mesh=mesh, in_specs=in_specs, out_specs=out_specs, check_vma=False)
```

profile of v0, /device:TPU:0, one launch (start us, length us, event | category | flops | bytes accessed | tf_op | source)
XLA Modules:
  0.0 159.1 jit_solution(11661200120718518420)
XLA Ops:
  6.5 0.0 copy-start
  6.5 0.0 all-gather.2.cloned.1.call-start
  6.5 0.7 all-gather.2.cloned.1.call-update
  7.3 0.0 reduce-scatter.2.cloned.1.call-start
  7.3 129.4 %all-gather.2.cloned.1.call-done = bf16[1,1024,4096]{2,1,0:T(8,128)(2,1)} async-done(((bf16[1,128,4096]{2,1,0:T(8,128)(2,1)}), bf16[1,1024,4096]{2,1,0:T(8,128)(2,1)}) %all-gather.2.cloned.1.call-update) | async-done | bytes 8388624 | tf_op jit(solution)/shard_map/all_gather | solution.py:12
  136.7 0.0 copy-done
  136.7 8.1 %fusion = f32[1024,384]{1,0:T(8,128)} fusion(bf16[1,1024,4096]{2,1,0:T(8,128)(2,1)} %all-gather.2.cloned.1.call-done, bf16[384,1,4096]{2,0,1:T(8,128)(2,1)S(1)} %copy-done), kind=kOutput, calls=%fused_computation | convolution fusion | flops 3221225472 | bytes 13107200 | tf_op jit(solution)/shard_map/lqk,nlk->qn/dot_general | solution.py:8
  144.8 0.0 reduce-scatter.2.cloned.1.call-update
  144.8 7.4 %reduce-scatter.2.cloned.1.call-done = f32[512,384]{1,0:T(8,128)} async-done(((f32[1024,384]{1,0:T(8,128)}), f32[512,384]{1,0:T(8,128)}) %reduce-scatter.2.cloned.1.call-update) | async-done | bytes 786448 | tf_op jit(solution)/shard_map/reduce_scatter | solution.py:13
Async XLA Ops:
  6.5 130.2 %copy-start = (bf16[384,1,4096]{2,0,1:T(8,128)(2,1)S(1)}, bf16[384,1,4096]{2,0,1:T(8,128)(2,1)}, u32[]{:S(2)}) copy-start(bf16[384,1,4096]{2,0,1:T(8,128)(2,1)} %param.2) | copy-start | bytes 9437188
  6.5 130.1 %all-gather.2.cloned.1.call-start = ((), (), s32[]{:S(2)}) async-start(), calls=%async_computation.1 | async-start | bytes 9437184 | tf_op jit(solution)/shard_map/all_gather | solution.py:12
  7.3 145.0 %reduce-scatter.2.cloned.1.call-start = ((), (), s32[]{:S(2)}) async-start(), calls=%async_computation.2 | async-start | bytes 2359296 | tf_op jit(solution)/shard_map/reduce_scatter | solution.py:13
Sparse Core Ops, SparseCore 0:
  9.5 127.1 all-gather.1
  145.0 7.2 reduce-scatter.1
where the time goes:
time: 159 us
  waiting for transfers between devices  137 us (86%)
  between operations  13.4 us (8%)
  matrix products  8.13 us (5%)
    all_gather x1, waiting for transfers between devices, shards(): lax.all_gather(query_grads, 'rows', axis=1, tiled=True)  129 us
    dot_general x1, matrix products, partial_scores(): jnp.einsum('lqk,nlk->qn', queries, train_grads, preferred_element_type=jn...  8.13 us
    reduce_scatter x1, waiting for transfers between devices, shards(): return lax.psum_scatter(terms, 'layers', scatter_dimension=0, tiled=True)  7.37 us
  transfers between devices with their start and end apart: 2, of which 2 were waited for; matrix products, arithmetic and copies ran while one was open for 0% of the time, Pallas kernels for 0%

commit v1 on v0

--- a/solution.py
+++ b/solution.py
@@ -2,6 +2,11 @@
 import jax.numpy as jnp
 from jax import lax
 from jax.sharding import PartitionSpec as P
+
+
+def swapped_in(value, axis, dim):
+    sent = jnp.stack([value] * lax.axis_size(axis))
+    return jnp.concatenate(lax.all_to_all(sent, axis, 0, 0), axis=dim)
 
 
 def partial_scores(queries, train_grads):
@@ -9,7 +14,7 @@
 
 
 def shards(train_grads, query_grads):
-    terms = partial_scores(lax.all_gather(query_grads, "rows", axis=1, tiled=True), train_grads)
+    terms = partial_scores(swapped_in(query_grads, "rows", 1), train_grads)
     return lax.psum_scatter(terms, "layers", scatter_dimension=0, tiled=True)
 
 

time: 159 us -> 220 us (1.38)
  blocking collectives: 0 us -> 190 us
  waiting for transfers between devices: 137 us -> 8.26 us
  matrix products: 8.13 us -> 5.67 us
  local copies, waits for them, and re-layouts: 0.01 us -> 2.42 us
    all_to_all x0 -> x1, blocking collectives: none -> 190 us  [swapped_in(): return jnp.concatenate(lax.all_to_all(sent, axis, 0, 0), axis=dim)]
    all_gather x1 -> x0, waiting for transfers between devices: 129 us -> none  [shards(): lax.all_gather(query_grads, 'rows', axis=1, tiled=True)]
    dot_general x1, matrix products: 8.13 us -> 5.67 us  [partial_scores(): jnp.einsum('lqk,nlk->qn', queries, train_grads, preferred_element_type=jn...]
    another operation x0 -> x1, local copies, waits for them, and re-layouts: none -> 2.41 us  [swapped_in(): sent = jnp.stack([value] * lax.axis_size(axis))]
  transfers between devices with their start and end apart: 2 -> 1, of which waited for: 2 -> 1; matrix products, arithmetic and copies ran while one was open for 0% -> 0% of each run, Pallas kernels for 0% -> 0%
where the time goes in v1:
time: 220 us
  blocking collectives  190 us (86%)
  between operations  13.4 us (6%)
  waiting for transfers between devices  8.26 us (4%)
  matrix products  5.67 us (3%)
  local copies, waits for them, and re-layouts  2.42 us (1%)
    all_to_all x1, blocking collectives, swapped_in(): return jnp.concatenate(lax.all_to_all(sent, axis, 0, 0), axis=dim)  190 us
    reduce_scatter x1, waiting for transfers between devices, shards(): return lax.psum_scatter(terms, 'layers', scatter_dimension=0, tiled=True)  8.24 us
    dot_general x1, matrix products, partial_scores(): jnp.einsum('lqk,nlk->qn', queries, train_grads, preferred_element_type=jn...  5.67 us
  transfers between devices with their start and end apart: 1, of which 1 were waited for; matrix products, arithmetic and copies ran while one was open for 0% of the time, Pallas kernels for 0%

profile of v1, /device:TPU:0, one launch (start us, length us, event | category | flops | bytes accessed | tf_op | source)
XLA Modules:
  0.0 219.9 jit_solution(1547742733377846307)
XLA Ops:
  6.5 0.0 copy-start
  6.5 0.0 reduce-scatter.2.cloned.1.call-start
  6.5 2.4 %stack.2 = bf16[8,1,128,4096]{3,2,1,0:T(8,128)(2,1)S(1)} broadcast(bf16[128,4096]{1,0:T(8,128)(2,1)} %bitcast.7), dimensions={2,3} | broadcast | bytes 9437184 | tf_op jit(solution)/shard_map/stack | solution.py:8
  9.0 190.1 %all_to_all.5 = bf16[8,1,128,4096]{3,2,1,0:T(8,128)(2,1)S(1)} all-to-all(bf16[8,1,128,4096]{3,2,1,0:T(8,128)(2,1)S(1)} %stack.2), channel_id=1, replica_groups=mesh['groups'=2,'rows'=8,'layers'=2] {'rows'}, dimensions={0} | all-to-all | bytes 16777216 | tf_op jit(solution)/shard_map/all_to_all | solution.py:9
  199.1 0.0 copy-done
  199.1 5.7 %fusion = f32[1024,384]{1,0:T(8,128)} fusion(bf16[1024,4096]{1,0:T(8,128)(2,1)S(1)} %bitcast.6, bf16[384,1,4096]{2,0,1:T(8,128)(2,1)S(1)} %copy-done), kind=kOutput, calls=%fused_computation | convolution fusion | flops 3221225472 | bytes 13107200 | tf_op jit(solution)/shard_map/lqk,nlk->qn/dot_general | solution.py:13
  204.8 0.0 reduce-scatter.2.cloned.1.call-update
  204.8 8.2 %reduce-scatter.2.cloned.1.call-done = f32[512,384]{1,0:T(8,128)} async-done(((f32[1024,384]{1,0:T(8,128)}), f32[512,384]{1,0:T(8,128)}) %reduce-scatter.2.cloned.1.call-update) | async-done | bytes 786448 | tf_op jit(solution)/shard_map/reduce_scatter | solution.py:18
Async XLA Ops:
  6.5 192.6 %copy-start = (bf16[384,1,4096]{2,0,1:T(8,128)(2,1)S(1)}, bf16[384,1,4096]{2,0,1:T(8,128)(2,1)}, u32[]{:S(2)}) copy-start(bf16[384,1,4096]{2,0,1:T(8,128)(2,1)} %param.2) | copy-start | bytes 9437188
  6.5 206.5 %reduce-scatter.2.cloned.1.call-start = ((), (), s32[]{:S(2)}) async-start(), calls=%async_computation.2 | async-start | bytes 2359296 | tf_op jit(solution)/shard_map/reduce_scatter | solution.py:18
Sparse Core Ops, SparseCore 0:
  204.9 8.0 reduce-scatter.1
